TPU v7x, 32 devices: a whole 2x2x4 slice. The times are simulated.
32 devices in a mesh: dom: 4 (over x, core), blk: 8 (over z, y).
Axes of the slice: x: 2, y: 2, z: 4, core: 2. Of those that a mesh axis runs over, the one named last changes fastest.
Arguments:
- ginv: float32 [4, 2048, 2048], P('dom', 'blk'), as said below
- couple: float32 [4, 2048, 2048], P('dom', 'blk'), may hold values from -0.109375 to 0.109375
- arrow_rhs: float32 [4, 64, 2048], P('dom', None, 'blk'), may hold values from -6 to 6
- arrow_in: float32 [64, 2048], P(None, 'blk'), may hold values from -6 to 6
- tip_cov: float32 [64, 64], replicated, as said below
- bnd_next: float32 [64, 2048], P(None, 'blk'), may hold values from -6 to 6
Outputs:
- arrow_rows: float32 [4, 64, 2048], P('dom', None, 'blk')
- cross_cov: float32 [4, 64, 2048], P('dom', None, 'blk')
Inputs may be any that keep to these rules, and one draw needn't show every extreme that they name: `ginv`: every block is zero above its diagonal, with diagonal entries between 0.5 and 1.5. `tip_cov`: Symmetric.
All inputs are finite; a program needn't handle non-finite values.
Results may differ from a plain program's by a relative error of at most 0.00013.
Values sent between devices are 32-bit elements; how exact they have to be, the bound alone decides.
A program may use at most 64 MiB of HBM per device.

v0:
```python
import jax
import jax.numpy as jnp
from jax import lax
from jax.sharding import PartitionSpec as P

highest = lax.Precision.HIGHEST


def passed_along(value, axis, steps):
    count = lax.axis_size(axis)
    first, last = (max(0, -steps), min(count, count - steps))
    return lax.ppermute(value, axis, [(source, source + steps) for source in range(first, last)])


def on_device(ginv, couple, arrow_rhs, arrow_in, tip_cov, bnd_next):
    g_rows = ginv[0]
    e_rows = couple[0]
    rhs_cols = arrow_rhs[0]
    panel_width = g_rows.shape[0]
    arrow_width = rhs_cols.shape[0]
    turn_count = lax.axis_size("dom")
    opening = lax.axis_index("dom") == 0
    closing = lax.axis_index("dom") == turn_count - 1

    def receive_rows(message):
        incoming = passed_along(message, "dom", 1)
        previous = jnp.where(opening, arrow_in, incoming)
        return lax.all_gather(previous, "blk", axis=1, tiled=True)

    def receive_later(message):
        incoming = passed_along(message, "dom", -1)
        return jnp.where(closing, bnd_next, incoming)

    def forward_turn(step_index, message):
        gathered = receive_rows(message)
        midway = rhs_cols - jnp.dot(gathered, e_rows.T, precision=highest)
        midway_whole = lax.all_gather(midway, "blk", axis=1, tiled=True)
        return jnp.dot(midway_whole, g_rows.T, precision=highest)

    arrow_local = lax.fori_loop(
        0, turn_count, forward_turn, jnp.zeros((arrow_width, panel_width), jnp.float32)
    )
    tip_term = jnp.dot(tip_cov, arrow_local, precision=highest)

    def backward_turn(step_index, state_pair):
        arriving = receive_later(state_pair[1])
        combined = arriving + tip_term
        covariance = lax.psum_scatter(
            -jnp.dot(combined, g_rows, precision=highest), "blk", scatter_dimension=1, tiled=True
        )
        onward = lax.psum_scatter(
            jnp.dot(covariance, e_rows, precision=highest), "blk", scatter_dimension=1, tiled=True
        )
        return (covariance, onward)

    empty = jnp.zeros((arrow_width, panel_width), jnp.float32)
    covariance, onward = lax.fori_loop(0, turn_count, backward_turn, (empty, empty))
    return (arrow_local[None], covariance[None])


def solution(mesh):
    return jax.shard_map(
        on_device,
        mesh=mesh,
        in_specs=(
            P("dom", "blk", None),
            P("dom", "blk", None),
            P("dom", None, "blk"),
            P(None, "blk"),
            P(),
            P(None, "blk"),
        ),
        out_specs=(P("dom", None, "blk"), P("dom", None, "blk")),
        check_vma=False,
    )
```

profile of v0, /device:TPU:0, one launch (start us, length us, event | category | flops | bytes accessed | tf_op | source)
XLA Modules:
  0.0 860.2 jit_solution(17411823055938083437)
XLA Ops:
  7.2 289.5 %while.22 = (s32[]{:T(128)}, f32[64,256]{1,0:T(8,128)S(1)}, pred[]{:T(512)}, f32[64,256]{1,0:T(8,128)}, f32[256,2048]{1,0:T(8,128)}, /*index=5*/f32[64,256]{1,0:T(8,128)}, f32[256,2048]{1,0:T(8,128)}, s32[]{:T(128)}) while((s32[]{:T(128)}, f32[64,256]{1,0:T(8,128)S(1)}, pred[]{:T(512)}, f32[64,256]{1,0:T(8,128)}, f32[256,2048]{1,0:T(8,128)}, ...), condition=%wide.region_1.2_spmd, body=%wide.region_0.1_spmd.sunk | while | flops 805339136 | bytes 15466650 | solution.py:40
  7.2 2.5 collective-permute-start
  9.8 0.9 collective-permute-done
  10.7 0.8 broadcast_select_fusion.2
  11.5 32.4 %all_gather.8 = f32[64,2048]{1,0:T(8,128)S(1)} all-gather(f32[64,256]{1,0:T(8,128)S(1)} %broadcast_select_fusion.2), channel_id=1, replica_groups=mesh['dom'=4,'blk'=8] {'blk'}, dimensions={1}, use_global_device_ids=true | all-gather | bytes 589824 | tf_op jit(solution)/shard_map/while/body/eval_jaxpr/all_gather | solution.py:28
  43.9 3.6 convolution_subtract_fusion.2
  47.5 31.4 %all_gather.9 = f32[64,2048]{1,0:T(8,128)S(1)} all-gather(f32[64,256]{1,0:T(8,128)S(1)} %convolution_subtract_fusion.2), channel_id=1, replica_groups=mesh['dom'=4,'blk'=8] {'blk'}, dimensions={1}, use_global_device_ids=true | all-gather | bytes 589824 | tf_op jit(solution)/shard_map/while/body/eval_jaxpr/all_gather | solution.py:37
  78.9 2.0 fusion.28
  81.0 1.4 collective-permute-start
  82.4 0.9 collective-permute-done
  83.3 0.8 broadcast_select_fusion.2
  84.1 31.7 %all_gather.8 = f32[64,2048]{1,0:T(8,128)S(1)} all-gather(f32[64,256]{1,0:T(8,128)S(1)} %broadcast_select_fusion.2), channel_id=1, replica_groups=mesh['dom'=4,'blk'=8] {'blk'}, dimensions={1}, use_global_device_ids=true | all-gather | bytes 589824 | tf_op jit(solution)/shard_map/while/body/eval_jaxpr/all_gather | solution.py:28
  115.8 3.6 convolution_subtract_fusion.2
  119.4 31.4 %all_gather.9 = f32[64,2048]{1,0:T(8,128)S(1)} all-gather(f32[64,256]{1,0:T(8,128)S(1)} %convolution_subtract_fusion.2), channel_id=1, replica_groups=mesh['dom'=4,'blk'=8] {'blk'}, dimensions={1}, use_global_device_ids=true | all-gather | bytes 589824 | tf_op jit(solution)/shard_map/while/body/eval_jaxpr/all_gather | solution.py:37
  150.8 2.0 fusion.28
  152.9 1.4 collective-permute-start
  154.3 0.9 collective-permute-done
  155.2 0.8 broadcast_select_fusion.2
  156.1 31.6 %all_gather.8 = f32[64,2048]{1,0:T(8,128)S(1)} all-gather(f32[64,256]{1,0:T(8,128)S(1)} %broadcast_select_fusion.2), channel_id=1, replica_groups=mesh['dom'=4,'blk'=8] {'blk'}, dimensions={1}, use_global_device_ids=true | all-gather | bytes 589824 | tf_op jit(solution)/shard_map/while/body/eval_jaxpr/all_gather | solution.py:28
  187.6 3.6 convolution_subtract_fusion.2
  191.3 31.5 %all_gather.9 = f32[64,2048]{1,0:T(8,128)S(1)} all-gather(f32[64,256]{1,0:T(8,128)S(1)} %convolution_subtract_fusion.2), channel_id=1, replica_groups=mesh['dom'=4,'blk'=8] {'blk'}, dimensions={1}, use_global_device_ids=true | all-gather | bytes 589824 | tf_op jit(solution)/shard_map/while/body/eval_jaxpr/all_gather | solution.py:37
  222.8 2.0 fusion.28
  224.9 1.4 collective-permute-start
  226.3 0.9 collective-permute-done
  227.2 0.8 broadcast_select_fusion.2
  228.0 31.5 %all_gather.8 = f32[64,2048]{1,0:T(8,128)S(1)} all-gather(f32[64,256]{1,0:T(8,128)S(1)} %broadcast_select_fusion.2), channel_id=1, replica_groups=mesh['dom'=4,'blk'=8] {'blk'}, dimensions={1}, use_global_device_ids=true | all-gather | bytes 589824 | tf_op jit(solution)/shard_map/while/body/eval_jaxpr/all_gather | solution.py:28
  259.5 3.6 convolution_subtract_fusion.2
  263.2 31.5 %all_gather.9 = f32[64,2048]{1,0:T(8,128)S(1)} all-gather(f32[64,256]{1,0:T(8,128)S(1)} %convolution_subtract_fusion.2), channel_id=1, replica_groups=mesh['dom'=4,'blk'=8] {'blk'}, dimensions={1}, use_global_device_ids=true | all-gather | bytes 589824 | tf_op jit(solution)/shard_map/while/body/eval_jaxpr/all_gather | solution.py:37
  294.7 2.0 fusion.28
  296.7 0.2 convolution_bitcast_fusion
  296.9 0.6 broadcast.3.clone.1
  297.6 0.6 broadcast.3
  298.2 555.1 %while.23 = (s32[]{:T(128)}, f32[64,256]{1,0:T(8,128)}, f32[64,256]{1,0:T(8,128)}, pred[]{:T(512)}, f32[64,256]{1,0:T(8,128)S(1)}, /*index=5*/f32[64,256]{1,0:T(...) while((s32[]{:T(128)}, f32[64,256]{1,0:T(8,128)}, f32[64,256]{1,0:T(8,128)}, pred[]{:T(512)}, ...), condition=%wide.region_5.6_spmd, body=%wide.region_2.5_spmd.sunk | while | flops 805470208 | bytes 17694960 | solution.py:57
  298.2 0.0 reduce-scatter.3.cloned.1.call-start
  298.3 1.4 collective-permute-start.1
  299.7 2.1 collective-permute-done.1
  301.7 3.8 convolution_negate_fusion.2
  305.5 0.0 reduce-scatter.5.cloned.1.call-start
  305.6 74.6 %reduce-scatter.3.cloned.1.call-done = f32[64,256]{1,0:T(8,128)} async-done(((f32[64,2048]{1,0:T(8,128)}), f32[64,256]{1,0:T(8,128)}) %reduce-scatter.3.cloned.1.call-update) | async-done | bytes 65552 | tf_op jit(solution)/shard_map/while/body/eval_jaxpr/reduce_scatter | solution.py:48
  380.2 3.0 fusion.33
  383.2 0.0 reduce-scatter.5.cloned.1.call-update
  383.2 62.4 %reduce-scatter.5.cloned.1.call-done = f32[64,256]{1,0:T(8,128)} async-done(((f32[64,2048]{1,0:T(8,128)}), f32[64,256]{1,0:T(8,128)}) %reduce-scatter.5.cloned.1.call-update) | async-done | bytes 65552 | tf_op jit(solution)/shard_map/while/body/eval_jaxpr/reduce_scatter | solution.py:51
  445.7 1.4 collective-permute-start.1
  447.1 2.1 collective-permute-done.1
  449.2 3.8 convolution_negate_fusion.2
  452.9 0.0 reduce-scatter.3.cloned.1.call-update
  452.9 0.0 reduce-scatter.5.cloned.1.call-start
  453.0 63.2 %reduce-scatter.3.cloned.1.call-done = f32[64,256]{1,0:T(8,128)} async-done(((f32[64,2048]{1,0:T(8,128)}), f32[64,256]{1,0:T(8,128)}) %reduce-scatter.3.cloned.1.call-update) | async-done | bytes 65552 | tf_op jit(solution)/shard_map/while/body/eval_jaxpr/reduce_scatter | solution.py:48
  516.2 3.0 fusion.33
  519.2 62.3 %reduce-scatter.5.cloned.1.call-done = f32[64,256]{1,0:T(8,128)} async-done(((f32[64,2048]{1,0:T(8,128)}), f32[64,256]{1,0:T(8,128)}) %reduce-scatter.5.cloned.1.call-update) | async-done | bytes 65552 | tf_op jit(solution)/shard_map/while/body/eval_jaxpr/reduce_scatter | solution.py:51
  581.6 1.4 collective-permute-start.1
  583.0 2.1 collective-permute-done.1
  585.1 3.8 convolution_negate_fusion.2
  588.8 0.0 reduce-scatter.5.cloned.1.call-start
  588.9 63.1 %reduce-scatter.3.cloned.1.call-done = f32[64,256]{1,0:T(8,128)} async-done(((f32[64,2048]{1,0:T(8,128)}), f32[64,256]{1,0:T(8,128)}) %reduce-scatter.3.cloned.1.call-update) | async-done | bytes 65552 | tf_op jit(solution)/shard_map/while/body/eval_jaxpr/reduce_scatter | solution.py:48
  652.0 3.0 fusion.33
  655.1 62.3 %reduce-scatter.5.cloned.1.call-done = f32[64,256]{1,0:T(8,128)} async-done(((f32[64,2048]{1,0:T(8,128)}), f32[64,256]{1,0:T(8,128)}) %reduce-scatter.5.cloned.1.call-update) | async-done | bytes 65552 | tf_op jit(solution)/shard_map/while/body/eval_jaxpr/reduce_scatter | solution.py:51
  717.3 1.4 collective-permute-start.1
  718.8 2.1 collective-permute-done.1
  720.8 3.8 convolution_negate_fusion.2
  724.6 0.0 reduce-scatter.5.cloned.1.call-start
  724.7 63.3 %reduce-scatter.3.cloned.1.call-done = f32[64,256]{1,0:T(8,128)} async-done(((f32[64,2048]{1,0:T(8,128)}), f32[64,256]{1,0:T(8,128)}) %reduce-scatter.3.cloned.1.call-update) | async-done | bytes 65552 | tf_op jit(solution)/shard_map/while/body/eval_jaxpr/reduce_scatter | solution.py:48
  787.9 3.0 fusion.33
  791.0 62.3 %reduce-scatter.5.cloned.1.call-done = f32[64,256]{1,0:T(8,128)} async-done(((f32[64,2048]{1,0:T(8,128)}), f32[64,256]{1,0:T(8,128)}) %reduce-scatter.5.cloned.1.call-update) | async-done | bytes 65552 | tf_op jit(solution)/shard_map/while/body/eval_jaxpr/reduce_scatter | solution.py:51
  (32 shorter events, 0.2 us)
Async XLA Ops:
  7.2 289.6 %copy-start = (f32[64,64]{1,0:T(8,128)S(1)}, f32[64,64]{1,0:T(8,128)}, u32[]{:S(2)}) copy-start(f32[64,64]{1,0:T(8,128)} %param.14) | copy-start | bytes 49156
  7.2 291.0 %copy-start.3 = (f32[64,256]{1,0:T(8,128)S(1)}, f32[64,256]{1,0:T(8,128)}, u32[]{:S(2)}) copy-start(f32[64,256]{1,0:T(8,128)} %param.15) | copy-start | bytes 196612
  7.2 71.7 %copy-start.2 = (f32[256,2048]{1,0:T(8,128)S(1)}, f32[256,2048]{1,0:T(8,128)}, u32[]{:S(2)}) copy-start(f32[256,2048]{1,0:T(8,128)} %get-tuple-element.224) | copy-start | bytes 6291460 | tf_op jit(solution)/shard_map/while
  7.2 3.4 collective-permute-start
  81.0 69.9 %copy-start.2 = (f32[256,2048]{1,0:T(8,128)S(1)}, f32[256,2048]{1,0:T(8,128)}, u32[]{:S(2)}) copy-start(f32[256,2048]{1,0:T(8,128)} %get-tuple-element.224) | copy-start | bytes 6291460 | tf_op jit(solution)/shard_map/while
  81.0 2.3 collective-permute-start
  152.9 69.9 %copy-start.2 = (f32[256,2048]{1,0:T(8,128)S(1)}, f32[256,2048]{1,0:T(8,128)}, u32[]{:S(2)}) copy-start(f32[256,2048]{1,0:T(8,128)} %get-tuple-element.224) | copy-start | bytes 6291460 | tf_op jit(solution)/shard_map/while
  152.9 2.3 collective-permute-start
  224.9 69.8 %copy-start.2 = (f32[256,2048]{1,0:T(8,128)S(1)}, f32[256,2048]{1,0:T(8,128)}, u32[]{:S(2)}) copy-start(f32[256,2048]{1,0:T(8,128)} %get-tuple-element.224) | copy-start | bytes 6291460 | tf_op jit(solution)/shard_map/while
  224.9 2.3 collective-permute-start
  296.7 1.5 copy-start.4
  298.2 82.0 %copy-start.1 = (f32[256,2048]{1,0:T(8,128)S(1)}, f32[256,2048]{1,0:T(8,128)}, u32[]{:S(2)}) copy-start(f32[256,2048]{1,0:T(8,128)} %get-tuple-element.251) | copy-start | bytes 6291460 | tf_op jit(solution)/shard_map/while
  298.2 82.0 %reduce-scatter.3.cloned.1.call-start = ((), (), s32[]{:S(2)}) async-start(), calls=%async_computation.2 | async-start | bytes 589824 | tf_op jit(solution)/shard_map/while/body/eval_jaxpr/reduce_scatter | solution.py:48
  298.3 3.5 collective-permute-start.1
  305.5 140.1 %reduce-scatter.5.cloned.1.call-start = ((), (), s32[]{:S(2)}) async-start(), calls=%async_computation.3 | async-start | bytes 589824 | tf_op jit(solution)/shard_map/while/body/eval_jaxpr/reduce_scatter | solution.py:51
  445.7 70.5 %copy-start.1 = (f32[256,2048]{1,0:T(8,128)S(1)}, f32[256,2048]{1,0:T(8,128)}, u32[]{:S(2)}) copy-start(f32[256,2048]{1,0:T(8,128)} %get-tuple-element.251) | copy-start | bytes 6291460 | tf_op jit(solution)/shard_map/while
  445.7 70.5 %reduce-scatter.3.cloned.1.call-start = ((), (), s32[]{:S(2)}) async-start(), calls=%async_computation.2 | async-start | bytes 589824 | tf_op jit(solution)/shard_map/while/body/eval_jaxpr/reduce_scatter | solution.py:48
  445.7 3.5 collective-permute-start.1
  452.9 128.6 %reduce-scatter.5.cloned.1.call-start = ((), (), s32[]{:S(2)}) async-start(), calls=%async_computation.3 | async-start | bytes 589824 | tf_op jit(solution)/shard_map/while/body/eval_jaxpr/reduce_scatter | solution.py:51
  581.6 70.4 %copy-start.1 = (f32[256,2048]{1,0:T(8,128)S(1)}, f32[256,2048]{1,0:T(8,128)}, u32[]{:S(2)}) copy-start(f32[256,2048]{1,0:T(8,128)} %get-tuple-element.251) | copy-start | bytes 6291460 | tf_op jit(solution)/shard_map/while
  581.6 70.4 %reduce-scatter.3.cloned.1.call-start = ((), (), s32[]{:S(2)}) async-start(), calls=%async_computation.2 | async-start | bytes 589824 | tf_op jit(solution)/shard_map/while/body/eval_jaxpr/reduce_scatter | solution.py:48
  581.6 3.5 collective-permute-start.1
  588.8 128.5 %reduce-scatter.5.cloned.1.call-start = ((), (), s32[]{:S(2)}) async-start(), calls=%async_computation.3 | async-start | bytes 589824 | tf_op jit(solution)/shard_map/while/body/eval_jaxpr/reduce_scatter | solution.py:51
  717.3 70.6 %copy-start.1 = (f32[256,2048]{1,0:T(8,128)S(1)}, f32[256,2048]{1,0:T(8,128)}, u32[]{:S(2)}) copy-start(f32[256,2048]{1,0:T(8,128)} %get-tuple-element.251) | copy-start | bytes 6291460 | tf_op jit(solution)/shard_map/while
  717.3 70.6 %reduce-scatter.3.cloned.1.call-start = ((), (), s32[]{:S(2)}) async-start(), calls=%async_computation.2 | async-start | bytes 589824 | tf_op jit(solution)/shard_map/while/body/eval_jaxpr/reduce_scatter | solution.py:48
  717.3 3.5 collective-permute-start.1
  724.6 128.7 %reduce-scatter.5.cloned.1.call-start = ((), (), s32[]{:S(2)}) async-start(), calls=%async_computation.3 | async-start | bytes 589824 | tf_op jit(solution)/shard_map/while/body/eval_jaxpr/reduce_scatter | solution.py:51
Sparse Core Ops, SparseCore 0:
  305.7 74.4 reduce-scatter.2
  383.5 62.1 reduce-scatter.4
  453.1 63.0 reduce-scatter.2
  519.4 62.1 reduce-scatter.4
  589.0 63.0 reduce-scatter.2
  655.2 62.0 reduce-scatter.4
  724.7 63.1 reduce-scatter.2
  791.3 61.9 reduce-scatter.4
where the time goes:
time: 861 us; the launch traced here: 860 us
  waiting for transfers between devices  525 us (61%)
  blocking collectives  253 us (29%)
  matrix products  50 us (6%)
  between operations  14.1 us (2%)
  starting transfers between devices  12.7 us (1%)
    reduce_scatter x4, waiting for transfers between devices, backward_turn(): lax.psum_scatter(-jnp.dot(combined, g_rows, precision=highest), 'blk', sc...  264 us
    reduce_scatter x4, waiting for transfers between devices, backward_turn(): lax.psum_scatter(jnp.dot(covariance, e_rows, precision=highest), 'blk', s...  249 us
    all_gather x4, blocking collectives, receive_rows(): return lax.all_gather(previous, 'blk', axis=1, tiled=True)  127 us
    all_gather x4, blocking collectives, forward_turn(): midway_whole = lax.all_gather(midway, 'blk', axis=1, tiled=True)  126 us
  transfers between devices with their start and end apart: 16, of which 16 were waited for; matrix products, arithmetic and copies ran while one was open for 0% of the time, Pallas kernels for 0%

commit v1 on v0

v1 whole, which is shorter than its diff:
```python
import functools

import jax
import jax.numpy as jnp
from jax import lax
from jax.experimental import pallas as pl
from jax.experimental.pallas import tpu as pltpu
from jax.sharding import PartitionSpec as P

CHUNKS = 2
MESH = pl.DeviceIdType.MESH
NT = (((1,), (1,)), ((), ()))
NN = (((1,), (0,)), ((), ()))


def halves(x):
    head = x.astype(jnp.bfloat16)
    rest = (x - head.astype(jnp.float32)).astype(jnp.bfloat16)
    return head, rest


def stacked(x):
    head, rest = halves(x)
    return jnp.concatenate([head, rest], axis=0)


def product(pair, w_head, w_rest, dims):
    rows = pair.shape[0] // 2
    both = lax.dot_general(pair, w_head, dims, preferred_element_type=jnp.float32)
    cross = lax.dot_general(pair[:rows], w_rest, dims, preferred_element_type=jnp.float32)
    return both[:rows] + (both[rows:] + cross)


def around(n):
    order = []
    for k in range(1, n // 2 + 1):
        order += [k] if k == n - k else [k, n - k]
    return order


def kernel(
    turns, n, chunks,
    g_hbm, e_hbm, rhs_hbm, ain_hbm, tip_hbm, bnd_hbm,
    rows_out, cov_out,
    g_raw, e_raw, g_head, g_rest, e_head, e_rest, rhs, tip, bnd,
    prev_in, mid_in, cov_in, on_in, mid_mine, row_mine, cov_part, on_part,
    load_sem, send_sem, recv_sem,
):
    t = lax.axis_index("dom")
    me = lax.axis_index("blk")
    a, w = rhs.shape
    part = a // chunks
    near = around(n)
    far = near[::-1]

    loads = [
        pltpu.make_async_copy(src, dst, load_sem.at[i])
        for i, (src, dst) in enumerate(
            [(e_hbm.at[0], e_raw), (rhs_hbm.at[0], rhs), (g_hbm.at[0], g_raw), (tip_hbm, tip), (bnd_hbm, bnd)]
        )
    ]
    for load in loads:
        load.start()

    barrier = pltpu.get_barrier_semaphore()

    def greet(dom, blk):
        pl.semaphore_signal(barrier, inc=1, device_id=(dom, blk), device_id_type=MESH)

    for k in near:
        greet(t, lax.rem(me + k, n))

    @pl.when(t > 0)
    def _():
        for k in range(n):
            greet(t - 1, lax.rem(me + k, n))

    @pl.when(t < turns - 1)
    def _():
        for k in range(n):
            greet(t + 1, lax.rem(me + k, n))

    def rows_of(c):
        return pl.ds(c * part, part)

    def send(stage, c, slot, src, dst, dst_sem, dom, blk):
        return pltpu.make_async_remote_copy(
            src_ref=src, dst_ref=dst, send_sem=send_sem.at[stage, c, slot], recv_sem=dst_sem,
            device_id=(dom, blk), device_id_type=MESH,
        )

    def arrived(stage, c, j, ref):
        pltpu.make_async_copy(ref.at[c, j], ref.at[c, j], recv_sem.at[stage, c, j]).wait()

    def arrow_copies(c):
        return [
            send(0, c, k, ain_hbm.at[rows_of(c)], prev_in.at[c, me], recv_sem.at[0, c, me], t, lax.rem(me + k, n))
            for k in far
        ]

    def own_arrow(c):
        return pltpu.make_async_copy(ain_hbm.at[rows_of(c)], prev_in.at[c, me], recv_sem.at[0, c, me])

    def mid_copy(c, k):
        return send(1, c, k, mid_mine.at[c], mid_in.at[c, me], recv_sem.at[1, c, me], t, me + k)

    def row_copies(c):
        return [
            send(2, c, k, row_mine.at[rows_of(c)], prev_in.at[c, me], recv_sem.at[0, c, me], t + 1, lax.rem(me + k, n))
            for k in far + [0]
        ]

    def cov_copy(c, k):
        return send(3, c, k, cov_part.at[c, me - k], cov_in.at[c, me], recv_sem.at[2, c, me], t, me - k)

    def on_copy(c, k):
        blk = lax.rem(me + k, n)
        return send(4, c, k, on_part.at[c, blk], on_in.at[c, me], recv_sem.at[3, c, me], t - 1, blk)

    greeted = n - 1 + n * jnp.where(t > 0, 1, 0) + n * jnp.where(t < turns - 1, 1, 0)
    pl.semaphore_wait(barrier, greeted)

    @pl.when(t == 0)
    def _():
        for c in range(chunks):
            own_arrow(c).start()
            for copy in arrow_copies(c):
                copy.start()

    loads[0].wait()
    for j in range(n):
        e_head[j], e_rest[j] = halves(e_raw[:, j * w:(j + 1) * w])
    loads[1].wait()
    loads[2].wait()
    for j in range(n):
        g_head[j], g_rest[j] = halves(g_raw[:, j * w:(j + 1) * w])
    loads[3].wait()
    loads[4].wait()

    for c in range(chunks):
        total = rhs[rows_of(c), :]
        for k in [0] + near:
            j = lax.rem(me + k, n)
            arrived(0, c, j, prev_in)
            total = total - product(stacked(prev_in[c, j]), e_head[j], e_rest[j], NT)
        mid_mine[c] = total
        for k in range(n - 1, 0, -1):
            @pl.when(me + k < n)
            def _(c=c, k=k):
                mid_copy(c, k).start()

    for c in range(chunks):
        row_mine[rows_of(c), :] = product(stacked(mid_mine[c]), g_head[me], g_rest[me], NT)
        for k in range(1, n):
            @pl.when(me - k >= 0)
            def _(c=c, k=k):
                j = me - k
                arrived(1, c, j, mid_in)
                row_mine[rows_of(c), :] += product(stacked(mid_in[c, j]), g_head[j], g_rest[j], NT)

        @pl.when(t < turns - 1)
        def _(c=c):
            for copy in row_copies(c):
                copy.start()

    rows_out[0] = row_mine[...]
    tip_term = jnp.dot(tip[...], row_mine[...], precision=lax.Precision.HIGHEST)
    bnd[...] = jnp.where(t == turns - 1, bnd[...], 0.0) + tip_term

    for c in range(chunks):
        @pl.when(t < turns - 1)
        def _(c=c):
            for k in [0] + near:
                j = lax.rem(me + k, n)
                arrived(3, c, j, on_in)
                bnd[rows_of(c), :] += on_in[c, j]

        pair = stacked(-bnd[rows_of(c), :])
        for k in range(n - 1, 0, -1):
            @pl.when(me - k >= 0)
            def _(c=c, k=k, pair=pair):
                j = me - k
                cov_part[c, j] = product(pair, g_head[j], g_rest[j], NN)
                cov_copy(c, k).start()
        cov_out[0, rows_of(c), :] = product(pair, g_head[me], g_rest[me], NN)

    for c in range(chunks):
        for k in range(1, n):
            @pl.when(me + k < n)
            def _(c=c, k=k):
                arrived(2, c, me + k, cov_in)
                cov_out[0, rows_of(c), :] += cov_in[c, me + k]

        @pl.when(t > 0)
        def _(c=c):
            pair = stacked(cov_out[0, rows_of(c), :])
            for k in far + [0]:
                j = lax.rem(me + k, n)
                on_part[c, j] = product(pair, e_head[j], e_rest[j], NN)
                on_copy(c, k).start()

    for c in range(chunks):
        @pl.when(t == 0)
        def _(c=c):
            for copy in arrow_copies(c):
                copy.wait_send()

        @pl.when(t < turns - 1)
        def _(c=c):
            for copy in row_copies(c):
                copy.wait_send()

        for k in range(1, n):
            @pl.when(me + k < n)
            def _(c=c, k=k):
                mid_copy(c, k).wait_send()

            @pl.when(me - k >= 0)
            def _(c=c, k=k):
                cov_copy(c, k).wait_send()

        @pl.when(t > 0)
        def _(c=c):
            for k in range(n):
                on_copy(c, k).wait_send()


def solution(mesh):
    turns, n = mesh.shape["dom"], mesh.shape["blk"]

    def on_device(ginv, couple, arrow_rhs, arrow_in, tip_cov, bnd_next):
        a, w = arrow_in.shape
        whole = ginv.shape[2]
        chunks = CHUNKS
        part = a // chunks
        f32, bf16 = jnp.float32, jnp.bfloat16
        shape = jax.ShapeDtypeStruct((1, a, w), f32)
        blocks = pltpu.VMEM((chunks, n, part, w), f32)
        split = pltpu.VMEM((n, w, w), bf16)
        rows, cov = pl.pallas_call(
            functools.partial(kernel, turns, n, chunks),
            out_shape=(shape, shape),
            in_specs=[pl.BlockSpec(memory_space=pl.ANY)] * 6,
            out_specs=(pl.BlockSpec(memory_space=pltpu.VMEM),) * 2,
            scratch_shapes=[
                pltpu.VMEM((w, whole), f32),
                pltpu.VMEM((w, whole), f32),
                split, split, split, split,
                pltpu.VMEM((a, w), f32),
                pltpu.VMEM((a, a), f32),
                pltpu.VMEM((a, w), f32),
                blocks, blocks, blocks, blocks,
                pltpu.VMEM((chunks, part, w), f32),
                pltpu.VMEM((a, w), f32),
                blocks, blocks,
                pltpu.SemaphoreType.DMA((5,)),
                pltpu.SemaphoreType.DMA((5, chunks, n)),
                pltpu.SemaphoreType.DMA((4, chunks, n)),
            ],
            compiler_params=pltpu.CompilerParams(
                collective_id=0, has_side_effects=True, vmem_limit_bytes=48 * 1024 * 1024
            ),
        )(ginv, couple, arrow_rhs, arrow_in, tip_cov, bnd_next)
        return rows, cov

    return jax.shard_map(
        on_device,
        mesh=mesh,
        in_specs=(
            P("dom", "blk", None),
            P("dom", "blk", None),
            P("dom", None, "blk"),
            P(None, "blk"),
            P(),
            P(None, "blk"),
        ),
        out_specs=(P("dom", None, "blk"), P("dom", None, "blk")),
        check_vma=False,
    )
```

time: 861 us -> 119 us (0.14)
  waiting for transfers between devices: 525 us -> 0 us
  blocking collectives: 253 us -> 0 us
  Pallas kernels: 0 us -> 110 us
  matrix products: 50 us -> 0 us
  between operations: 14.1 us -> 0.65 us
  starting transfers between devices: 12.7 us -> 0 us
    reduce_scatter x8 -> x0, waiting for transfers between devices: 514 us -> none  [the longest x4 264 us: backward_turn(): lax.psum_scatter(-jnp.dot(combined, g_rows, precision=highest), 'blk', sc...]
    all_gather x8 -> x0, blocking collectives: 253 us -> none  [the longest x4 127 us: receive_rows(): return lax.all_gather(previous, 'blk', axis=1, tiled=True)]
    pallas_call x0 -> x1, Pallas kernels: none -> 110 us  [on_device(): pl.pallas_call(functools.partial(kernel, turns, n, chunks), out_shape=(sh...]
    dot_general x17 -> x0, matrix products: 50 us -> none  [the longest x4 15.1 us: backward_turn(): jnp.dot(combined, g_rows, precision=highest)]
    ppermute x8 -> x0, starting transfers between devices: 12.5 us -> none  [passed_along(): lax.ppermute(value, axis, [(source, source + steps) for source in range(f...]
    ppermute x8 -> x0, waiting for transfers between devices: 11.8 us -> none  [passed_along(): lax.ppermute(value, axis, [(source, source + steps) for source in range(f...]
  transfers between devices with their start and end apart: 16 -> 0, of which waited for: 16 -> 0; matrix products, arithmetic and copies ran while one was open for 0% -> 0% of each run, Pallas kernels for 0% -> 0%
where the time goes in v1:
time: 119 us
  Pallas kernels  110 us (92%)
  local copies, waits for them, and re-layouts  7.71 us (6%)
    pallas_call x1, Pallas kernels, on_device(): pl.pallas_call(functools.partial(kernel, turns, n, chunks), out_shape=(sh...  110 us
    unnamed x14, local copies, waits for them, and re-layouts  7.71 us

profile of v1, /device:TPU:0, one launch (start us, length us, event | category | flops | bytes accessed | tf_op | source)
XLA Modules:
  0.0 118.5 jit_solution(15484424057625487346)
XLA Ops:
  0.6 0.0 copy-start
  0.6 1.6 %copy-done = f32[1,256,2048]{2,1,0:T(8,128)S(1)} copy-done((f32[1,256,2048]{2,1,0:T(8,128)S(1)}, f32[1,256,2048]{2,1,0:T(8,128)}, u32[]{:S(2)}) %copy-start) | copy-done | bytes 2097176
  2.2 0.0 copy-start.1
  2.2 1.6 %copy-done.1 = f32[1,256,2048]{2,1,0:T(8,128)S(1)} copy-done((f32[1,256,2048]{2,1,0:T(8,128)S(1)}, f32[1,256,2048]{2,1,0:T(8,128)}, u32[]{:S(2)}) %copy-start.1) | copy-done | bytes 2097176
  3.8 0.0 copy-start.2
  3.8 0.8 copy-done.2
  4.7 0.0 copy-start.3
  4.7 0.8 copy-done.3
  5.5 0.0 copy-start.4
  5.5 0.8 copy-done.4
  6.3 0.0 copy-start.5
  6.3 0.8 copy-done.5
  7.1 110.1 %shard_map.77 = (f32[1,64,256]{2,1,0:T(8,128)S(1)}, f32[1,64,256]{2,1,0:T(8,128)S(1)}) custom-call(f32[1,256,2048]{2,1,0:T(8,128)S(1)} %copy-done, f32[1,256,2048]{2,1,0:T(8,128)S(1)} %copy-done.1, f32[1,64,256]{2,1,0:T(8,128)S(1)} %copy-done.2, f32[64,256]{1,0:T(8,128)S(1)} %copy-done.3, f32[64,64]{1,0:T(8,128)S(1)} %copy-done.5, f32[64,256]{1,0:T(8,128)S(1)} %copy-done.4), custom_call_target="tpu_custom_call" | custom-call | tf_op jit(solution)/shard_map/pallas_call | solution.py:240
  117.2 0.6 copy.10
  117.9 0.6 copy.11
Async XLA Ops:
  0.6 1.6 %copy-start = (f32[1,256,2048]{2,1,0:T(8,128)S(1)}, f32[1,256,2048]{2,1,0:T(8,128)}, u32[]{:S(2)}) copy-start(f32[1,256,2048]{2,1,0:T(8,128)} %g_hbm.1) | copy-start | bytes 6291460
  2.2 1.6 %copy-start.1 = (f32[1,256,2048]{2,1,0:T(8,128)S(1)}, f32[1,256,2048]{2,1,0:T(8,128)}, u32[]{:S(2)}) copy-start(f32[1,256,2048]{2,1,0:T(8,128)} %e_hbm.1) | copy-start | bytes 6291460
  3.8 0.8 copy-start.2
  4.7 0.8 copy-start.3
  5.5 0.8 copy-start.4
  6.3 0.8 copy-start.5

commit v2 on v1

--- a/solution.py
+++ b/solution.py
@@ -8,6 +8,15 @@
 from jax.sharding import PartitionSpec as P
 
 CHUNKS = 2
+
+
+def ORDER(pairs):
+    return range(1, pairs)
+
+
+def PUT(routes, side):
+    return [side] + routes
+
 MESH = pl.DeviceIdType.MESH
 NT = (((1,), (1,)), ((), ()))
 NN = (((1,), (0,)), ((), ()))
@@ -51,7 +60,20 @@
     a, w = rhs.shape
     part = a // chunks
     near = around(n)
-    far = near[::-1]
+    pairs = n // 2
+    p, y = lax.div(me, 2), lax.rem(me, 2)
+    buddy = me + 1 - 2 * y
+    before, after = t - 1, t + 1
+    up, down, full = [], [], []
+    for d in ORDER(pairs):
+        for across in (1, 0):
+            high = (p + d < pairs, 2 * (p + d) + (1 - y if across else y))
+            low = (p - d >= 0, 2 * (p - d) + (1 - y if across else y))
+            up.append(high)
+            down.append(low)
+            full += [high, low]
+    side = (y >= 0, buddy)
+    up, down, full = PUT(up, (y == 0, buddy)), PUT(down, (y == 1, buddy)), PUT(full, side)
 
     loads = [
         pltpu.make_async_copy(src, dst, load_sem.at[i])
@@ -92,30 +114,33 @@
     def arrived(stage, c, j, ref):
         pltpu.make_async_copy(ref.at[c, j], ref.at[c, j], recv_sem.at[stage, c, j]).wait()
 
-    def arrow_copies(c):
-        return [
-            send(0, c, k, ain_hbm.at[rows_of(c)], prev_in.at[c, me], recv_sem.at[0, c, me], t, lax.rem(me + k, n))
-            for k in far
-        ]
-
     def own_arrow(c):
         return pltpu.make_async_copy(ain_hbm.at[rows_of(c)], prev_in.at[c, me], recv_sem.at[0, c, me])
 
-    def mid_copy(c, k):
-        return send(1, c, k, mid_mine.at[c], mid_in.at[c, me], recv_sem.at[1, c, me], t, me + k)
-
-    def row_copies(c):
-        return [
-            send(2, c, k, row_mine.at[rows_of(c)], prev_in.at[c, me], recv_sem.at[0, c, me], t + 1, lax.rem(me + k, n))
-            for k in far + [0]
-        ]
-
-    def cov_copy(c, k):
-        return send(3, c, k, cov_part.at[c, me - k], cov_in.at[c, me], recv_sem.at[2, c, me], t, me - k)
-
-    def on_copy(c, k):
-        blk = lax.rem(me + k, n)
-        return send(4, c, k, on_part.at[c, blk], on_in.at[c, me], recv_sem.at[3, c, me], t - 1, blk)
+    def arrow_copy(c, blk):
+        return send(0, c, blk, ain_hbm.at[rows_of(c)], prev_in.at[c, me], recv_sem.at[0, c, me], t, blk)
+
+    def mid_copy(c, blk):
+        return send(1, c, blk, mid_mine.at[c], mid_in.at[c, me], recv_sem.at[1, c, me], t, blk)
+
+    def row_copy(c, blk):
+        return send(2, c, blk, row_mine.at[rows_of(c)], prev_in.at[c, me], recv_sem.at[0, c, me], after, blk)
+
+    def cov_copy(c, blk):
+        return send(3, c, blk, cov_part.at[c, blk], cov_in.at[c, me], recv_sem.at[2, c, me], t, blk)
+
+    def on_copy(c, blk):
+        return send(4, c, blk, on_part.at[c, blk], on_in.at[c, me], recv_sem.at[3, c, me], before, blk)
+
+    def each(routes, body):
+        for guard, blk in routes:
+            pl.when(guard)(functools.partial(body, blk))
+
+    def start(copy, c):
+        return lambda blk: copy(c, blk).start()
+
+    def left(copy, c):
+        return lambda blk: copy(c, blk).wait_send()
 
     greeted = n - 1 + n * jnp.where(t > 0, 1, 0) + n * jnp.where(t < turns - 1, 1, 0)
     pl.semaphore_wait(barrier, greeted)
@@ -124,8 +149,7 @@
     def _():
         for c in range(chunks):
             own_arrow(c).start()
-            for copy in arrow_copies(c):
-                copy.start()
+            each(full, start(arrow_copy, c))
 
     loads[0].wait()
     for j in range(n):
@@ -144,10 +168,7 @@
             arrived(0, c, j, prev_in)
             total = total - product(stacked(prev_in[c, j]), e_head[j], e_rest[j], NT)
         mid_mine[c] = total
-        for k in range(n - 1, 0, -1):
-            @pl.when(me + k < n)
-            def _(c=c, k=k):
-                mid_copy(c, k).start()
+        each(up, start(mid_copy, c))
 
     for c in range(chunks):
         row_mine[rows_of(c), :] = product(stacked(mid_mine[c]), g_head[me], g_rest[me], NT)
@@ -160,8 +181,8 @@
 
         @pl.when(t < turns - 1)
         def _(c=c):
-            for copy in row_copies(c):
-                copy.start()
+            each(full, start(row_copy, c))
+            row_copy(c, me).start()
 
     rows_out[0] = row_mine[...]
     tip_term = jnp.dot(tip[...], row_mine[...], precision=lax.Precision.HIGHEST)
@@ -176,12 +197,10 @@
                 bnd[rows_of(c), :] += on_in[c, j]
 
         pair = stacked(-bnd[rows_of(c), :])
-        for k in range(n - 1, 0, -1):
-            @pl.when(me - k >= 0)
-            def _(c=c, k=k, pair=pair):
-                j = me - k
-                cov_part[c, j] = product(pair, g_head[j], g_rest[j], NN)
-                cov_copy(c, k).start()
+        def give_cov(j, c=c, pair=pair):
+            cov_part[c, j] = product(pair, g_head[j], g_rest[j], NN)
+            cov_copy(c, j).start()
+        each(down, give_cov)
         cov_out[0, rows_of(c), :] = product(pair, g_head[me], g_rest[me], NN)
 
     for c in range(chunks):
@@ -194,35 +213,30 @@
         @pl.when(t > 0)
         def _(c=c):
             pair = stacked(cov_out[0, rows_of(c), :])
-            for k in far + [0]:
-                j = lax.rem(me + k, n)
+
+            def give_on(j):
                 on_part[c, j] = product(pair, e_head[j], e_rest[j], NN)
-                on_copy(c, k).start()
+                on_copy(c, j).start()
+            each(full, give_on)
+            give_on(me)
 
     for c in range(chunks):
         @pl.when(t == 0)
         def _(c=c):
-            for copy in arrow_copies(c):
-                copy.wait_send()
+            each(full, left(arrow_copy, c))
 
         @pl.when(t < turns - 1)
         def _(c=c):
-            for copy in row_copies(c):
-                copy.wait_send()
-
-        for k in range(1, n):
-            @pl.when(me + k < n)
-            def _(c=c, k=k):
-                mid_copy(c, k).wait_send()
-
-            @pl.when(me - k >= 0)
-            def _(c=c, k=k):
-                cov_copy(c, k).wait_send()
+            each(full, left(row_copy, c))
+            left(row_copy, c)(me)
+
+        each(up, left(mid_copy, c))
+        each(down, left(cov_copy, c))
 
         @pl.when(t > 0)
         def _(c=c):
-            for k in range(n):
-                on_copy(c, k).wait_send()
+            each(full, left(on_copy, c))
+            left(on_copy, c)(me)
 
 
 def solution(mesh):

time: 119 us -> 112 us (0.941)
  Pallas kernels: 110 us -> 103 us
    pallas_call x1, Pallas kernels: 110 us -> 103 us  [on_device(): pl.pallas_call(functools.partial(kernel, turns, n, chunks), out_shape=(sh...]
where the time goes in v2:
time: 112 us
  Pallas kernels  103 us (92%)
  local copies, waits for them, and re-layouts  7.71 us (7%)
    pallas_call x1, Pallas kernels, on_device(): pl.pallas_call(functools.partial(kernel, turns, n, chunks), out_shape=(sh...  103 us
    unnamed x14, local copies, waits for them, and re-layouts  7.71 us

profile of v2, /device:TPU:0, one launch (start us, length us, event | category | flops | bytes accessed | tf_op | source)
XLA Modules:
  0.0 111.7 jit_solution(959290456948873849)
XLA Ops:
  0.6 0.0 copy-start
  0.6 1.6 %copy-done = f32[1,256,2048]{2,1,0:T(8,128)S(1)} copy-done((f32[1,256,2048]{2,1,0:T(8,128)S(1)}, f32[1,256,2048]{2,1,0:T(8,128)}, u32[]{:S(2)}) %copy-start) | copy-done | bytes 2097176
  2.2 0.0 copy-start.1
  2.2 1.6 %copy-done.1 = f32[1,256,2048]{2,1,0:T(8,128)S(1)} copy-done((f32[1,256,2048]{2,1,0:T(8,128)S(1)}, f32[1,256,2048]{2,1,0:T(8,128)}, u32[]{:S(2)}) %copy-start.1) | copy-done | bytes 2097176
  3.8 0.0 copy-start.2
  3.8 0.8 copy-done.2
  4.7 0.0 copy-start.3
  4.7 0.8 copy-done.3
  5.5 0.0 copy-start.4
  5.5 0.8 copy-done.4
  6.3 0.0 copy-start.5
  6.3 0.8 copy-done.5
  7.1 103.3 %shard_map.77 = (f32[1,64,256]{2,1,0:T(8,128)S(1)}, f32[1,64,256]{2,1,0:T(8,128)S(1)}) custom-call(f32[1,256,2048]{2,1,0:T(8,128)S(1)} %copy-done, f32[1,256,2048]{2,1,0:T(8,128)S(1)} %copy-done.1, f32[1,64,256]{2,1,0:T(8,128)S(1)} %copy-done.2, f32[64,256]{1,0:T(8,128)S(1)} %copy-done.3, f32[64,64]{1,0:T(8,128)S(1)} %copy-done.5, f32[64,256]{1,0:T(8,128)S(1)} %copy-done.4), custom_call_target="tpu_custom_call" | custom-call | tf_op jit(solution)/shard_map/pallas_call | solution.py:254
  110.4 0.6 copy.10
  111.1 0.6 copy.11
Async XLA Ops:
  0.6 1.6 %copy-start = (f32[1,256,2048]{2,1,0:T(8,128)S(1)}, f32[1,256,2048]{2,1,0:T(8,128)}, u32[]{:S(2)}) copy-start(f32[1,256,2048]{2,1,0:T(8,128)} %g_hbm.1) | copy-start | bytes 6291460
  2.2 1.6 %copy-start.1 = (f32[1,256,2048]{2,1,0:T(8,128)S(1)}, f32[1,256,2048]{2,1,0:T(8,128)}, u32[]{:S(2)}) copy-start(f32[1,256,2048]{2,1,0:T(8,128)} %e_hbm.1) | copy-start | bytes 6291460
  3.8 0.8 copy-start.2
  4.7 0.8 copy-start.3
  5.5 0.8 copy-start.4
  6.3 0.8 copy-start.5

commit v3 on v2

--- a/solution.py
+++ b/solution.py
@@ -65,8 +65,8 @@
     buddy = me + 1 - 2 * y
     before, after = t - 1, t + 1
     up, down, full = [], [], []
-    for d in ORDER(pairs):
-        for across in (1, 0):
+    for across in (1, 0):
+        for d in ORDER(pairs):
             high = (p + d < pairs, 2 * (p + d) + (1 - y if across else y))
             low = (p - d >= 0, 2 * (p - d) + (1 - y if across else y))
             up.append(high)
@@ -162,22 +162,22 @@
     loads[4].wait()
 
     for c in range(chunks):
-        total = rhs[rows_of(c), :]
-        for k in [0] + near:
-            j = lax.rem(me + k, n)
+        mid_mine[c] = rhs[rows_of(c), :]
+
+        def take_prev(j, c=c):
             arrived(0, c, j, prev_in)
-            total = total - product(stacked(prev_in[c, j]), e_head[j], e_rest[j], NT)
-        mid_mine[c] = total
+            mid_mine[c] -= product(stacked(prev_in[c, j]), e_head[j], e_rest[j], NT)
+        take_prev(me)
+        each(full, take_prev)
         each(up, start(mid_copy, c))
 
     for c in range(chunks):
         row_mine[rows_of(c), :] = product(stacked(mid_mine[c]), g_head[me], g_rest[me], NT)
-        for k in range(1, n):
-            @pl.when(me - k >= 0)
-            def _(c=c, k=k):
-                j = me - k
-                arrived(1, c, j, mid_in)
-                row_mine[rows_of(c), :] += product(stacked(mid_in[c, j]), g_head[j], g_rest[j], NT)
+
+        def take_mid(j, c=c):
+            arrived(1, c, j, mid_in)
+            row_mine[rows_of(c), :] += product(stacked(mid_in[c, j]), g_head[j], g_rest[j], NT)
+        each(down, take_mid)
 
         @pl.when(t < turns - 1)
         def _(c=c):
@@ -272,7 +272,7 @@
                 pltpu.SemaphoreType.DMA((4, chunks, n)),
             ],
             compiler_params=pltpu.CompilerParams(
-                collective_id=0, has_side_effects=True, vmem_limit_bytes=48 * 1024 * 1024
+                collective_id=0, has_side_effects=True
             ),
         )(ginv, couple, arrow_rhs, arrow_in, tip_cov, bnd_next)
         return rows, cov

time: 112 us -> 103 us (0.920)
  local copies, waits for them, and re-layouts: 7.71 us -> 2.95 us
  Pallas kernels: 103 us -> 99 us
    unnamed x14 -> x2, local copies, waits for them, and re-layouts: 7.71 us -> 2.95 us
    pallas_call x1, Pallas kernels: 103 us -> 99 us  [on_device(): pl.pallas_call(functools.partial(kernel, turns, n, chunks), out_shape=(sh...]
where the time goes in v3:
time: 103 us
  Pallas kernels  99 us (96%)
  local copies, waits for them, and re-layouts  2.95 us (3%)
    pallas_call x1, Pallas kernels, on_device(): pl.pallas_call(functools.partial(kernel, turns, n, chunks), out_shape=(sh...  99 us
    unnamed x2, local copies, waits for them, and re-layouts  2.95 us

profile of v3, /device:TPU:0, one launch (start us, length us, event | category | flops | bytes accessed | tf_op | source)
XLA Modules:
  0.0 102.6 jit_solution(18332628084949603198)
XLA Ops:
  0.6 99.0 %shard_map.77 = (f32[1,64,256]{2,1,0:T(8,128)}, f32[1,64,256]{2,1,0:T(8,128)}) custom-call(f32[1,256,2048]{2,1,0:T(8,128)} %g_hbm.1, f32[1,256,2048]{2,1,0:T(8,128)} %e_hbm.1, f32[1,64,256]{2,1,0:T(8,128)} %rhs_hbm.1, f32[64,256]{1,0:T(8,128)} %ain_hbm.1, f32[64,64]{1,0:T(8,128)} %tip_hbm.1, f32[64,256]{1,0:T(8,128)} %bnd_hbm.1), custom_call_target="tpu_custom_call" | custom-call | tf_op jit(solution)/shard_map/pallas_call | solution.py:254
  99.6 1.5 %copy.10 = f32[1,64,256]{2,1,0:T(8,128)} copy(f32[1,64,256]{2,1,0:T(8,128)} %get-tuple-element.4) | data formatting | bytes 131072
  101.1 1.5 %copy.11 = f32[1,64,256]{2,1,0:T(8,128)} copy(f32[1,64,256]{2,1,0:T(8,128)} %get-tuple-element.5) | data formatting | bytes 131072
